TPU v7x, 256 devices: a whole 4x4x8 slice. The times are simulated.
256 devices in a mesh: rep: 32 (over y, z), shard: 8 (over x, core).
Axes of the slice: x: 4, y: 4, z: 8, core: 2. Of those that a mesh axis runs over, the one named last changes fastest.
Arguments:
- gradient: bfloat16 [32, 1024, 4096], P('rep', None, 'shard'), may hold values from -16 to 16
- feedback: bfloat16 [32, 1024, 4096], P('rep', None, 'shard'), may hold values from -4 to 4
- warm_start: float32 [1024, 64], replicated, may hold values from -6 to 6
- master: float32 [1024, 4096], P('rep', 'shard'), may hold values from -4 to 4
- moment: float32 [1024, 4096], P('rep', 'shard'), may hold values from -1.5 to 1.5
- second: float32 [1024, 4096], P('rep', 'shard'), may hold values from 0.005 to 0.5
Outputs:
- new_feedback: bfloat16 [32, 1024, 4096], P('rep', None, 'shard')
- weights: bfloat16 [1024, 4096], P(None, 'shard')
- master_out: float32 [1024, 4096], P('rep', 'shard')
- moment_out: float32 [1024, 4096], P('rep', 'shard')
- second_out: float32 [1024, 4096], P('rep', 'shard')
- right_factor: float32 [1024, 64], replicated
All inputs are finite; a program needn't handle non-finite values.
Results may differ from a plain program's by a relative error of at most 0.001.
Values may be sent and summed in bfloat16 or wider, within the bound.
No kernel may reach another device: no remote copies, remote signals or barrier semaphores. Data moves between devices by JAX's collectives and lax.ppermute only.
A program may use at most 64 MiB of HBM per device.

v0:
```python
import jax
import jax.numpy as jnp
from jax import lax
from jax.sharding import PartitionSpec as P

HIGHEST = lax.Precision.HIGHEST
beta_one = 0.9
beta_two = 0.95
learn_rate = 0.02
decay_rate = 0.1
adam_eps = 1e-08
ridge_rate = 1e-06


def lower_inverse(gram):
    matrix_order = gram.shape[0]
    identity = jnp.eye(matrix_order, dtype=jnp.float32)
    ridge_term = ridge_rate * jnp.trace(gram) / matrix_order
    cholesky_lower = jnp.linalg.cholesky(gram + ridge_term * identity)
    return jax.scipy.linalg.solve_triangular(cholesky_lower, identity, lower=True)


def contract_first(left, right):
    return lax.dot_general(
        left, right, (((0,), (0,)), ((), ())), precision=HIGHEST, preferred_element_type=jnp.float32
    )


def times_inverse(left, inverse):
    return jnp.dot(left, inverse.T, precision=HIGHEST, preferred_element_type=jnp.float32)


def on_device(gradient, feedback, warm_start, master, moment, second):
    replicas = lax.axis_size("rep")
    merged = gradient[0].astype(jnp.float32) + feedback[0].astype(jnp.float32)
    local_factor = contract_first(merged, warm_start)
    factor = lax.psum(local_factor, "rep") / replicas
    gram_part = contract_first(factor, factor)
    gram = lax.psum(gram_part, "shard")
    inverse = lower_inverse(gram)
    unit_basis = times_inverse(factor, inverse)
    projected = jnp.dot(merged, unit_basis, precision=HIGHEST, preferred_element_type=jnp.float32)
    right_factor = lax.psum(projected, ("rep", "shard")) / replicas
    approx = lax.dot_general(
        right_factor,
        unit_basis,
        (((1,), (1,)), ((), ())),
        precision=HIGHEST,
        preferred_element_type=jnp.float32,
    )
    new_feedback = (merged - approx).astype(jnp.bfloat16)[None]
    own_rows = master.shape[0]
    row_start = lax.axis_index("rep") * own_rows
    grad_rows = lax.dynamic_slice_in_dim(approx, row_start, own_rows, 0)
    moment_out = beta_one * moment + (1.0 - beta_one) * grad_rows
    second_out = beta_two * second + (1.0 - beta_two) * grad_rows * grad_rows
    master_out = master - learn_rate * (
        moment_out / (jnp.sqrt(second_out) + adam_eps) + decay_rate * master
    )
    weights = lax.all_gather(master_out.astype(jnp.bfloat16), "rep", axis=0, tiled=True)
    return (new_feedback, weights, master_out, moment_out, second_out, right_factor)


def solution(mesh):
    return jax.shard_map(
        on_device,
        mesh=mesh,
        in_specs=(
            P("rep", None, "shard"),
            P("rep", None, "shard"),
            P(),
            P("rep", "shard"),
            P("rep", "shard"),
            P("rep", "shard"),
        ),
        out_specs=(
            P("rep", None, "shard"),
            P(None, "shard"),
            P("rep", "shard"),
            P("rep", "shard"),
            P("rep", "shard"),
            P(),
        ),
        check_vma=False,
    )
```

profile of v0, /device:TPU:2, one launch (start us, length us, event | category | flops | bytes accessed | tf_op | source)
XLA Modules:
  0.0 533.7 jit_solution(15276774667782180067)
XLA Ops:
  7.2 0.9 copy-done
  8.1 3.8 fusion.2
  12.0 0.0 all-reduce.5.cloned.1.call-start
  12.0 143.7 %all-reduce.3.cloned.1.call-done = f32[512,64]{0,1:T(8,128)} async-done(((f32[512,64]{0,1:T(8,128)}), f32[512,64]{0,1:T(8,128)}) %all-reduce.3.cloned.1.call-update) | async-done | bytes 131088 | tf_op jit(solution)/shard_map/psum | solution.py:37
  155.8 1.2 fusion.8
  157.0 20.7 %psum.22 = f32[64,64]{1,0:T(8,128)S(1)} all-reduce(f32[64,64]{1,0:T(8,128)S(1)} %fusion.8), channel_id=1, replica_groups=mesh['rep'=32,'shard'=8] {'shard'}, use_global_device_ids=true, to_apply=%region_1.0 | all-reduce | flops 4096 | bytes 32768 | tf_op jit(solution)/shard_map/psum | solution.py:39
  177.7 0.6 select_reduce_fusion.1
  179.0 0.1 copy.12
  179.1 5.8 %cholesky.18 = f32[64,64]{1,0:T(8,128)S(1)} custom-call(f32[64,64]{1,0:T(8,128)S(1)} %fusion.16), custom_call_target="Cholesky" | custom-call | tf_op jit(solution)/shard_map/jit(cholesky)/cholesky | solution.py:19
  185.0 0.6 compare_reduce_fusion
  185.6 0.7 fusion.13
  186.3 4.9 custom-call.7
  191.2 0.2 fusion.14
  191.4 1.2 fusion.6
  192.6 3.0 fusion
  195.7 0.0 all-gather.2.cloned.1.call-start
  195.7 249.2 %all-reduce.5.cloned.1.call-done = f32[1024,64]{0,1:T(8,128)} async-done(((f32[1024,64]{0,1:T(8,128)}), f32[1024,64]{0,1:T(8,128)}) %all-reduce.5.cloned.1.call-update) | async-done | bytes 262160 | tf_op jit(solution)/shard_map/psum | solution.py:43
  444.9 1.0 broadcast_multiply_fusion
  445.9 1.8 fusion.21
  447.8 1.3 copy-done.3
  449.1 0.7 fusion.19
  449.9 3.0 fusion.5
  452.9 72.0 %all-gather.2.cloned.1.call-done = bf16[1024,512]{1,0:T(8,128)(2,1)} async-done(((bf16[32,512]{1,0:T(8,128)(2,1)}), bf16[1024,512]{1,0:T(8,128)(2,1)}) %all-gather.2.cloned.1.call-update) | async-done | bytes 1048592 | tf_op jit(solution)/shard_map/all_gather | solution.py:60
  524.9 2.3 copy.16
  (21 shorter events, 0.2 us)
Async XLA Ops:
  7.2 1.0 copy-start
  7.2 185.4 %copy-start.1 = (bf16[1,1024,512]{2,1,0:T(8,128)(2,1)S(1)}, bf16[1,1024,512]{2,1,0:T(8,128)(2,1)}, u32[]{:S(2)}) copy-start(bf16[1,1024,512]{2,1,0:T(8,128)(2,1)} %param.7) | copy-start | bytes 3145732
  7.2 185.4 %copy-start.2 = (bf16[1,1024,512]{2,1,0:T(8,128)(2,1)S(1)}, bf16[1,1024,512]{2,1,0:T(8,128)(2,1)}, u32[]{:S(2)}) copy-start(bf16[1,1024,512]{2,1,0:T(8,128)(2,1)} %param.6) | copy-start | bytes 3145732
  7.2 148.6 %all-reduce.3.cloned.1.call-start = ((), (), s32[]{:S(2)}) async-start(), calls=%async_computation | async-start | bytes 262144 | tf_op jit(solution)/shard_map/psum | solution.py:37
  12.0 432.9 %all-reduce.5.cloned.1.call-start = ((), (), s32[]{:S(2)}) async-start(), calls=%async_computation.1 | async-start | bytes 524288 | tf_op jit(solution)/shard_map/psum | solution.py:43
  195.6 253.5 %copy-start.5 = (f32[32,512]{1,0:T(8,128)S(1)}, f32[32,512]{1,0:T(8,128)}, u32[]{:S(2)}) copy-start(f32[32,512]{1,0:T(8,128)} %param.9) | copy-start | bytes 196612
  195.6 253.5 %copy-start.6 = (f32[32,512]{1,0:T(8,128)S(1)}, f32[32,512]{1,0:T(8,128)}, u32[]{:S(2)}) copy-start(f32[32,512]{1,0:T(8,128)} %param.11) | copy-start | bytes 196612
  195.6 253.5 %copy-start.7 = (f32[32,512]{1,0:T(8,128)S(1)}, f32[32,512]{1,0:T(8,128)}, u32[]{:S(2)}) copy-start(f32[32,512]{1,0:T(8,128)} %param.10) | copy-start | bytes 196612
  195.7 329.2 %all-gather.2.cloned.1.call-start = ((), (), s32[]{:S(2)}) async-start(), calls=%async_computation.2 | async-start | bytes 1081344 | tf_op jit(solution)/shard_map/all_gather | solution.py:60
  445.9 7.0 %copy-start.4 = (f32[1024,64]{0,1:T(8,128)}, f32[1024,64]{0,1:T(8,128)S(1)}, u32[]{:S(2)}) copy-start(f32[1024,64]{0,1:T(8,128)S(1)} %broadcast_multiply_fusion) | copy-start | bytes 786436
  447.8 1.3 copy-start.3
Sparse Core Ops, SparseCore 0:
  12.1 143.6 all-reduce.2
  195.8 249.0 all-reduce.4
  450.0 74.8 all-gather.1
where the time goes:
time: 534 us
  waiting for transfers between devices  465 us (87%)
  blocking collectives  20.7 us (4%)
  other arithmetic  17.4 us (3%)
  between operations  14.5 us (3%)
  matrix products  11.4 us (2%)
    psum x1, waiting for transfers between devices, on_device(): right_factor = lax.psum(projected, ('rep', 'shard')) / replicas  249 us
    psum x1, waiting for transfers between devices, on_device(): factor = lax.psum(local_factor, 'rep') / replicas  144 us
    all_gather x1, waiting for transfers between devices, on_device(): lax.all_gather(master_out.astype(jnp.bfloat16), 'rep', axis=0, tiled=True)  72 us
    psum x1, blocking collectives, on_device(): gram = lax.psum(gram_part, 'shard')  20.7 us
  transfers between devices with their start and end apart: 3, of which 3 were waited for; matrix products, arithmetic and copies ran while one was open for 1% of the time, Pallas kernels for 0%

commit v1 on v0

--- a/solution.py
+++ b/solution.py
@@ -40,7 +40,7 @@
     inverse = lower_inverse(gram)
     unit_basis = times_inverse(factor, inverse)
     projected = jnp.dot(merged, unit_basis, precision=HIGHEST, preferred_element_type=jnp.float32)
-    right_factor = lax.psum(projected, ("rep", "shard")) / replicas
+    right_factor = lax.psum(lax.psum(projected, "rep"), "shard") / replicas
     approx = lax.dot_general(
         right_factor,
         unit_basis,

time: 534 us -> 493 us (0.923)
  waiting for transfers between devices: 465 us -> 424 us
    psum x1 -> x2, waiting for transfers between devices: 249 us -> 205 us  [on_device(): right_factor = lax.psum(lax.psum(projected, 'rep'), 'shard') / replicas]
  transfers between devices with their start and end apart: 3 -> 4, of which waited for: 3 -> 4; matrix products, arithmetic and copies ran while one was open for 1% -> 1% of each run, Pallas kernels for 0% -> 0%
where the time goes in v1:
time: 493 us; the launch traced here: 492 us
  waiting for transfers between devices  424 us (86%)
  blocking collectives  20.7 us (4%)
  other arithmetic  17.4 us (4%)
  between operations  14.5 us (3%)
  matrix products  11.4 us (2%)
    psum x2, waiting for transfers between devices, on_device(): right_factor = lax.psum(lax.psum(projected, 'rep'), 'shard') / replicas  205 us
    psum x1, waiting for transfers between devices, on_device(): factor = lax.psum(local_factor, 'rep') / replicas  144 us
    all_gather x1, waiting for transfers between devices, on_device(): lax.all_gather(master_out.astype(jnp.bfloat16), 'rep', axis=0, tiled=True)  74.6 us
    psum x1, blocking collectives, on_device(): gram = lax.psum(gram_part, 'shard')  20.7 us
  transfers between devices with their start and end apart: 4, of which 4 were waited for; matrix products, arithmetic and copies ran while one was open for 1% of the time, Pallas kernels for 0%

profile of v1, /device:TPU:2, one launch (start us, length us, event | category | flops | bytes accessed | tf_op | source)
XLA Modules:
  0.0 492.3 jit_solution(14507239277692262874)
XLA Ops:
  7.2 0.9 copy-done
  8.1 3.8 fusion.2
  12.0 0.0 all-reduce.6.cloned.1.call-start
  12.0 143.7 %all-reduce.4.cloned.1.call-done = f32[512,64]{0,1:T(8,128)} async-done(((f32[512,64]{0,1:T(8,128)}), f32[512,64]{0,1:T(8,128)}) %all-reduce.4.cloned.1.call-update) | async-done | bytes 131088 | tf_op jit(solution)/shard_map/psum | solution.py:37
  155.8 1.2 fusion.8
  157.0 20.7 %psum.29 = f32[64,64]{1,0:T(8,128)S(1)} all-reduce(f32[64,64]{1,0:T(8,128)S(1)} %fusion.8), channel_id=1, replica_groups=mesh['rep'=32,'shard'=8] {'shard'}, use_global_device_ids=true, to_apply=%region_1.0 | all-reduce | flops 4096 | bytes 32768 | tf_op jit(solution)/shard_map/psum | solution.py:39
  177.7 0.6 select_reduce_fusion.1
  179.0 0.1 copy.12
  179.1 5.8 %cholesky.18 = f32[64,64]{1,0:T(8,128)S(1)} custom-call(f32[64,64]{1,0:T(8,128)S(1)} %fusion.16), custom_call_target="Cholesky" | custom-call | tf_op jit(solution)/shard_map/jit(cholesky)/cholesky | solution.py:19
  185.0 0.6 compare_reduce_fusion
  185.6 0.7 fusion.13
  186.3 4.9 custom-call.7
  191.2 0.2 fusion.14
  191.4 1.2 fusion.6
  192.6 3.0 fusion
  195.7 143.0 %all-reduce.6.cloned.1.call-done = f32[1024,64]{0,1:T(8,128)} async-done(((f32[1024,64]{0,1:T(8,128)}), f32[1024,64]{0,1:T(8,128)}) %all-reduce.6.cloned.1.call-update) | async-done | bytes 262160 | tf_op jit(solution)/shard_map/psum | solution.py:43
  338.8 62.1 %all-reduce.8.cloned.1.call-done = f32[1024,64]{0,1:T(8,128)} async-done(((f32[1024,64]{0,1:T(8,128)}), f32[1024,64]{0,1:T(8,128)}) %all-reduce.8.cloned.1.call-update) | async-done | bytes 262160 | tf_op jit(solution)/shard_map/psum | solution.py:43
  400.9 1.0 broadcast_multiply_fusion
  401.9 1.8 fusion.21
  403.7 1.3 copy-done.3
  405.1 0.7 fusion.19
  405.8 3.0 fusion.5
  408.8 74.6 %all-gather.2.cloned.1.call-done = bf16[1024,512]{1,0:T(8,128)(2,1)} async-done(((bf16[32,512]{1,0:T(8,128)(2,1)}), bf16[1024,512]{1,0:T(8,128)(2,1)}) %all-gather.2.cloned.1.call-update) | async-done | bytes 1048592 | tf_op jit(solution)/shard_map/all_gather | solution.py:60
  483.5 2.3 copy.17
  (24 shorter events, 0.3 us)
Async XLA Ops:
  7.2 1.0 copy-start
  7.2 185.4 %copy-start.1 = (bf16[1,1024,512]{2,1,0:T(8,128)(2,1)S(1)}, bf16[1,1024,512]{2,1,0:T(8,128)(2,1)}, u32[]{:S(2)}) copy-start(bf16[1,1024,512]{2,1,0:T(8,128)(2,1)} %param.7) | copy-start | bytes 3145732
  7.2 185.4 %copy-start.2 = (bf16[1,1024,512]{2,1,0:T(8,128)(2,1)S(1)}, bf16[1,1024,512]{2,1,0:T(8,128)(2,1)}, u32[]{:S(2)}) copy-start(bf16[1,1024,512]{2,1,0:T(8,128)(2,1)} %param.6) | copy-start | bytes 3145732
  7.2 148.6 %all-reduce.4.cloned.1.call-start = ((), (), s32[]{:S(2)}) async-start(), calls=%async_computation | async-start | bytes 262144 | tf_op jit(solution)/shard_map/psum | solution.py:37
  12.0 326.8 %all-reduce.6.cloned.1.call-start = ((), (), s32[]{:S(2)}) async-start(), calls=%async_computation.1 | async-start | bytes 524288 | tf_op jit(solution)/shard_map/psum | solution.py:43
  195.6 209.4 %copy-start.5 = (f32[32,512]{1,0:T(8,128)S(1)}, f32[32,512]{1,0:T(8,128)}, u32[]{:S(2)}) copy-start(f32[32,512]{1,0:T(8,128)} %param.9) | copy-start | bytes 196612
  195.6 209.4 %copy-start.6 = (f32[32,512]{1,0:T(8,128)S(1)}, f32[32,512]{1,0:T(8,128)}, u32[]{:S(2)}) copy-start(f32[32,512]{1,0:T(8,128)} %param.11) | copy-start | bytes 196612
  195.6 209.4 %copy-start.7 = (f32[32,512]{1,0:T(8,128)S(1)}, f32[32,512]{1,0:T(8,128)}, u32[]{:S(2)}) copy-start(f32[32,512]{1,0:T(8,128)} %param.10) | copy-start | bytes 196612
  195.7 205.2 %all-reduce.8.cloned.1.call-start = ((), (), s32[]{:S(2)}) async-start(), calls=%async_computation.2 | async-start | bytes 524288 | tf_op jit(solution)/shard_map/psum | solution.py:43
  338.8 144.7 %all-gather.2.cloned.1.call-start = ((), (), s32[]{:S(2)}) async-start(), calls=%async_computation.3 | async-start | bytes 1081344 | tf_op jit(solution)/shard_map/all_gather | solution.py:60
  401.9 7.0 %copy-start.4 = (f32[1024,64]{0,1:T(8,128)}, f32[1024,64]{0,1:T(8,128)S(1)}, u32[]{:S(2)}) copy-start(f32[1024,64]{0,1:T(8,128)S(1)} %broadcast_multiply_fusion) | copy-start | bytes 786436
  403.7 1.3 copy-start.3
Sparse Core Ops, SparseCore 0:
  12.1 143.6 all-reduce.3
  195.8 142.9 all-reduce.5
  341.2 59.6 all-reduce.7
  405.9 77.4 all-gather.1

commit v2 on v0

--- a/solution.py
+++ b/solution.py
@@ -34,7 +34,7 @@
     replicas = lax.axis_size("rep")
     merged = gradient[0].astype(jnp.float32) + feedback[0].astype(jnp.float32)
     local_factor = contract_first(merged, warm_start)
-    factor = lax.psum(local_factor, "rep") / replicas
+    factor = jnp.sum(lax.all_gather(local_factor, "rep"), axis=0) / replicas
     gram_part = contract_first(factor, factor)
     gram = lax.psum(gram_part, "shard")
     inverse = lower_inverse(gram)

time: 534 us -> 477 us (0.89)
  waiting for transfers between devices: 465 us -> 405 us
    psum x1 -> x0, waiting for transfers between devices: 144 us -> none  [on_device(): factor = lax.psum(local_factor, 'rep') / replicas]
    all_gather x0 -> x1, waiting for transfers between devices: none -> 84.9 us  [on_device(): factor = jnp.sum(lax.all_gather(local_factor, 'rep'), axis=0) / replicas]
where the time goes in v2:
time: 477 us
  waiting for transfers between devices  405 us (85%)
  blocking collectives  20.7 us (4%)
  other arithmetic  18.1 us (4%)
  between operations  14.5 us (3%)
  matrix products  9.48 us (2%)
  local copies, waits for them, and re-layouts  9.17 us (2%)
    psum x1, waiting for transfers between devices, on_device(): right_factor = lax.psum(projected, ('rep', 'shard')) / replicas  248 us
    all_gather x1, waiting for transfers between devices, on_device(): factor = jnp.sum(lax.all_gather(local_factor, 'rep'), axis=0) / replicas  84.9 us
    all_gather x1, waiting for transfers between devices, on_device(): lax.all_gather(master_out.astype(jnp.bfloat16), 'rep', axis=0, tiled=True)  72 us
    psum x1, blocking collectives, on_device(): gram = lax.psum(gram_part, 'shard')  20.7 us
  transfers between devices with their start and end apart: 3, of which 3 were waited for; matrix products, arithmetic and copies ran while one was open for 1% of the time, Pallas kernels for 0%

profile of v2, /device:TPU:2, one launch (start us, length us, event | category | flops | bytes accessed | tf_op | source)
XLA Modules:
  0.0 476.9 jit_solution(3839892153477366375)
XLA Ops:
  7.2 0.9 copy-done
  8.1 3.8 fusion.2
  12.0 84.9 %all-gather.6.cloned.1.call-done = f32[16384,64]{0,1:T(8,128)} async-done(((f32[512,64]{0,1:T(8,128)}), f32[16384,64]{0,1:T(8,128)}) %all-gather.6.cloned.1.call-update) | async-done | bytes 4194320 | tf_op jit(solution)/shard_map/all_gather | solution.py:37
  96.9 4.6 copy.14
  101.5 0.7 bitcast_reduce_fusion
  102.2 0.3 fusion.8
  102.4 20.7 %psum.14 = f32[64,64]{1,0:T(8,128)S(1)} all-reduce(f32[64,64]{1,0:T(8,128)S(1)} %fusion.8), channel_id=1, replica_groups=mesh['rep'=32,'shard'=8] {'shard'}, use_global_device_ids=true, to_apply=%region_1.0 | all-reduce | flops 4096 | bytes 32768 | tf_op jit(solution)/shard_map/psum | solution.py:39
  123.1 0.6 select_reduce_fusion.1
  124.4 0.1 copy.13
  124.5 5.8 %cholesky.18 = f32[64,64]{1,0:T(8,128)S(1)} custom-call(f32[64,64]{1,0:T(8,128)S(1)} %fusion.16), custom_call_target="Cholesky" | custom-call | tf_op jit(solution)/shard_map/jit(cholesky)/cholesky | solution.py:19
  130.4 0.6 compare_reduce_fusion
  131.0 0.7 fusion.13
  131.7 4.9 %custom-call.7 = f32[1,64,64]{1,2,0:T(8,128)S(1)} custom-call(f32[1,64,64]{2,1,0:T(8,128)S(1)} %fusion.13), custom_call_target="InvertDiagBlocksLowerTriangular" | custom-call | tf_op jit(solution)/shard_map/jit(_solve_triangular)/triangular_solve | solution.py:20
  136.6 0.2 fusion.14
  136.8 0.3 fusion.6
  137.1 3.0 fusion
  140.2 248.0 %all-reduce.2.cloned.1.call-done = f32[1024,64]{0,1:T(8,128)} async-done(((f32[1024,64]{0,1:T(8,128)}), f32[1024,64]{0,1:T(8,128)}) %all-reduce.2.cloned.1.call-update) | async-done | bytes 262160 | tf_op jit(solution)/shard_map/psum | solution.py:43
  388.2 1.0 broadcast_multiply_fusion
  389.2 1.8 fusion.21
  391.1 1.3 copy-done.3
  392.4 0.7 fusion.19
  393.1 3.0 fusion.5
  396.2 72.0 %all-gather.4.cloned.1.call-done = bf16[1024,512]{1,0:T(8,128)(2,1)} async-done(((bf16[32,512]{1,0:T(8,128)(2,1)}), bf16[1024,512]{1,0:T(8,128)(2,1)}) %all-gather.4.cloned.1.call-update) | async-done | bytes 1048592 | tf_op jit(solution)/shard_map/all_gather | solution.py:60
  468.1 2.3 copy.17
  (23 shorter events, 0.3 us)
Async XLA Ops:
  7.2 1.0 copy-start
  7.2 89.7 %all-gather.6.cloned.1.call-start = ((), (), s32[]{:S(2)}) async-start(), calls=%async_computation.2 | async-start | bytes 4325376 | tf_op jit(solution)/shard_map/all_gather | solution.py:37
  12.0 376.2 %all-reduce.2.cloned.1.call-start = ((), (), s32[]{:S(2)}) async-start(), calls=%async_computation | async-start | bytes 524288 | tf_op jit(solution)/shard_map/psum | solution.py:43
  101.5 35.6 %copy-start.1 = (bf16[1,1024,512]{2,1,0:T(8,128)(2,1)S(1)}, bf16[1,1024,512]{2,1,0:T(8,128)(2,1)}, u32[]{:S(2)}) copy-start(bf16[1,1024,512]{2,1,0:T(8,128)(2,1)} %param.7) | copy-start | bytes 3145732
  101.5 35.6 %copy-start.2 = (bf16[1,1024,512]{2,1,0:T(8,128)(2,1)S(1)}, bf16[1,1024,512]{2,1,0:T(8,128)(2,1)}, u32[]{:S(2)}) copy-start(bf16[1,1024,512]{2,1,0:T(8,128)(2,1)} %param.6) | copy-start | bytes 3145732
  140.1 252.3 %copy-start.5 = (f32[32,512]{1,0:T(8,128)S(1)}, f32[32,512]{1,0:T(8,128)}, u32[]{:S(2)}) copy-start(f32[32,512]{1,0:T(8,128)} %param.9) | copy-start | bytes 196612
  140.2 252.3 %copy-start.6 = (f32[32,512]{1,0:T(8,128)S(1)}, f32[32,512]{1,0:T(8,128)}, u32[]{:S(2)}) copy-start(f32[32,512]{1,0:T(8,128)} %param.11) | copy-start | bytes 196612
  140.2 252.3 %copy-start.7 = (f32[32,512]{1,0:T(8,128)S(1)}, f32[32,512]{1,0:T(8,128)}, u32[]{:S(2)}) copy-start(f32[32,512]{1,0:T(8,128)} %param.10) | copy-start | bytes 196612
  140.2 328.0 %all-gather.4.cloned.1.call-start = ((), (), s32[]{:S(2)}) async-start(), calls=%async_computation.1 | async-start | bytes 1081344 | tf_op jit(solution)/shard_map/all_gather | solution.py:60
  389.2 7.0 %copy-start.4 = (f32[1024,64]{0,1:T(8,128)}, f32[1024,64]{0,1:T(8,128)S(1)}, u32[]{:S(2)}) copy-start(f32[1024,64]{0,1:T(8,128)S(1)} %broadcast_multiply_fusion) | copy-start | bytes 786436
  391.1 1.3 copy-start.3
Sparse Core Ops, SparseCore 0:
  12.1 84.7 all-gather.5
  140.3 247.8 all-reduce.1
  393.3 74.8 all-gather.3

commit v3 on v0

--- a/solution.py
+++ b/solution.py
@@ -57,7 +57,12 @@
     master_out = master - learn_rate * (
         moment_out / (jnp.sqrt(second_out) + adam_eps) + decay_rate * master
     )
-    weights = lax.all_gather(master_out.astype(jnp.bfloat16), "rep", axis=0, tiled=True)
+    weights = jnp.concatenate(
+        lax.all_to_all(
+            jnp.stack([master_out.astype(jnp.bfloat16)] * lax.axis_size("rep")), "rep", 0, 0
+        ),
+        axis=0,
+    )
     return (new_feedback, weights, master_out, moment_out, second_out, right_factor)
 
 

time: 534 us -> 496 us (0.929)
  waiting for transfers between devices: 465 us -> 418 us
  starting transfers between devices: 0.12 us -> 7.31 us
    all_gather x1 -> x0, waiting for transfers between devices: 72 us -> none  [on_device(): lax.all_gather(master_out.astype(jnp.bfloat16), 'rep', axis=0, tiled=True)]
    all_to_all x0 -> x1, waiting for transfers between devices: none -> 24.8 us  [on_device(): lax.all_to_all(jnp.stack([master_out.astype(jnp.bfloat16)] * lax.axis_siz...]
    all_to_all x0 -> x1, starting transfers between devices: none -> 7.23 us  [on_device(): lax.all_to_all(jnp.stack([master_out.astype(jnp.bfloat16)] * lax.axis_siz...]
where the time goes in v3:
time: 496 us; the launch traced here: 494 us
  waiting for transfers between devices  418 us (84%)
  blocking collectives  20.7 us (4%)
  other arithmetic  17.4 us (4%)
  between operations  14.8 us (3%)
  matrix products  11.3 us (2%)
  starting transfers between devices  7.31 us (1%)
    psum x1, waiting for transfers between devices, on_device(): right_factor = lax.psum(projected, ('rep', 'shard')) / replicas  249 us
    psum x1, waiting for transfers between devices, on_device(): factor = lax.psum(local_factor, 'rep') / replicas  144 us
    all_to_all x1, waiting for transfers between devices, on_device(): lax.all_to_all(jnp.stack([master_out.astype(jnp.bfloat16)] * lax.axis_siz...  24.8 us
    psum x1, blocking collectives, on_device(): gram = lax.psum(gram_part, 'shard')  20.7 us
  transfers between devices with their start and end apart: 3, of which 3 were waited for; matrix products, arithmetic and copies ran while one was open for 1% of the time, Pallas kernels for 0%

profile of v3, /device:TPU:2, one launch (start us, length us, event | category | flops | bytes accessed | tf_op | source)
XLA Modules:
  0.0 493.8 jit_solution(13463714889890789120)
XLA Ops:
  7.2 0.9 copy-done
  8.1 3.8 fusion.2
  12.0 143.7 %all-reduce.3.cloned.1.call-done = f32[512,64]{0,1:T(8,128)} async-done(((f32[512,64]{0,1:T(8,128)}), f32[512,64]{0,1:T(8,128)}) %all-reduce.3.cloned.1.call-update) | async-done | bytes 131088 | tf_op jit(solution)/shard_map/psum | solution.py:37
  155.8 1.2 fusion.8
  157.0 20.7 %psum.22 = f32[64,64]{1,0:T(8,128)S(1)} all-reduce(f32[64,64]{1,0:T(8,128)S(1)} %fusion.8), channel_id=1, replica_groups=mesh['rep'=32,'shard'=8] {'shard'}, use_global_device_ids=true, to_apply=%region_1.0 | all-reduce | flops 4096 | bytes 32768 | tf_op jit(solution)/shard_map/psum | solution.py:39
  177.7 0.6 select_reduce_fusion.1
  179.0 0.1 copy.12
  179.1 5.8 %cholesky.18 = f32[64,64]{1,0:T(8,128)S(1)} custom-call(f32[64,64]{1,0:T(8,128)S(1)} %fusion.16), custom_call_target="Cholesky" | custom-call | tf_op jit(solution)/shard_map/jit(cholesky)/cholesky | solution.py:19
  185.0 0.6 compare_reduce_fusion
  185.6 0.7 fusion.13
  186.3 4.9 custom-call.7
  191.2 0.2 fusion.14
  191.4 1.2 fusion.6
  192.6 3.0 fusion
  195.7 249.2 %all-reduce.5.cloned.1.call-done = f32[1024,64]{0,1:T(8,128)} async-done(((f32[1024,64]{0,1:T(8,128)}), f32[1024,64]{0,1:T(8,128)}) %all-reduce.5.cloned.1.call-update) | async-done | bytes 262160 | tf_op jit(solution)/shard_map/psum | solution.py:43
  444.9 1.0 broadcast_multiply_fusion
  445.9 1.8 fusion.21
  447.7 1.3 copy-done.3
  449.1 0.7 fusion.19
  449.8 1.1 stack.2
  450.9 7.2 %all-to-all-start = ((bf16[32,32,512]{2,1,0:T(8,128)(2,1)}), bf16[32,32,512]{2,1,0:T(8,128)(2,1)S(1)}, u32[]{:S(2)}, u32[]{:S(2)}) async-start(bf16[32,32,512]{2,1,0:T(8,128)(2,1)} %stack.2), calls=%async_computation | async-start | bytes 2097152 | tf_op jit(solution)/shard_map/all_to_all | solution.py:61
  458.1 3.0 fusion.5
  461.1 24.8 %all-to-all-done = bf16[32,32,512]{2,1,0:T(8,128)(2,1)S(1)} async-done(((bf16[32,32,512]{2,1,0:T(8,128)(2,1)}), bf16[32,32,512]{2,1,0:T(8,128)(2,1)S(1)}, u32[]{:S(2)}, u32[]{:S(2)}) %all-to-all-start) | async-done | bytes 1048608 | tf_op jit(solution)/shard_map/all_to_all | solution.py:61
  486.0 1.0 copy.16
  (21 shorter events, 0.2 us)
Async XLA Ops:
  7.2 1.0 copy-start
  7.2 185.4 %copy-start.1 = (bf16[1,1024,512]{2,1,0:T(8,128)(2,1)S(1)}, bf16[1,1024,512]{2,1,0:T(8,128)(2,1)}, u32[]{:S(2)}) copy-start(bf16[1,1024,512]{2,1,0:T(8,128)(2,1)} %param.7) | copy-start | bytes 3145732
  7.2 185.4 %copy-start.2 = (bf16[1,1024,512]{2,1,0:T(8,128)(2,1)S(1)}, bf16[1,1024,512]{2,1,0:T(8,128)(2,1)}, u32[]{:S(2)}) copy-start(bf16[1,1024,512]{2,1,0:T(8,128)(2,1)} %param.6) | copy-start | bytes 3145732
  7.2 148.6 %all-reduce.3.cloned.1.call-start = ((), (), s32[]{:S(2)}) async-start(), calls=%async_computation.1 | async-start | bytes 262144 | tf_op jit(solution)/shard_map/psum | solution.py:37
  12.0 432.9 %all-reduce.5.cloned.1.call-start = ((), (), s32[]{:S(2)}) async-start(), calls=%async_computation.2 | async-start | bytes 524288 | tf_op jit(solution)/shard_map/psum | solution.py:43
  195.6 253.4 %copy-start.5 = (f32[32,512]{1,0:T(8,128)S(1)}, f32[32,512]{1,0:T(8,128)}, u32[]{:S(2)}) copy-start(f32[32,512]{1,0:T(8,128)} %param.9) | copy-start | bytes 196612
  195.6 253.4 %copy-start.6 = (f32[32,512]{1,0:T(8,128)S(1)}, f32[32,512]{1,0:T(8,128)}, u32[]{:S(2)}) copy-start(f32[32,512]{1,0:T(8,128)} %param.11) | copy-start | bytes 196612
  195.6 253.4 %copy-start.7 = (f32[32,512]{1,0:T(8,128)S(1)}, f32[32,512]{1,0:T(8,128)}, u32[]{:S(2)}) copy-start(f32[32,512]{1,0:T(8,128)} %param.10) | copy-start | bytes 196612
  445.8 3.9 copy-start.4
  447.7 1.4 copy-start.3
  450.9 35.1 %all-to-all-start = ((bf16[32,32,512]{2,1,0:T(8,128)(2,1)}), bf16[32,32,512]{2,1,0:T(8,128)(2,1)S(1)}, u32[]{:S(2)}, u32[]{:S(2)}) async-start(bf16[32,32,512]{2,1,0:T(8,128)(2,1)} %stack.2), calls=%async_computation | async-start | bytes 2097152 | tf_op jit(solution)/shard_map/all_to_all | solution.py:61
Sparse Core Ops, SparseCore 0:
  12.1 143.6 all-reduce.2
  195.8 249.0 all-reduce.4
